TPU v7x, 32 devices: a whole 2x2x4 slice. The times are simulated.
32 devices in a mesh: expert: 2 (over x), seq: 4 (over z), fsdp: 4 (over y, core).
Axes of the slice: x: 2, y: 2, z: 4, core: 2. Of those that a mesh axis runs over, the one named last changes fastest.
Arguments:
- queries: bfloat16 [16384, 5120], P(('expert', 'seq', 'fsdp')), parts along dimension 0, may hold values from -100 to 100
- keys: bfloat16 [16384, 5120], P(('expert', 'seq', 'fsdp')), parts along dimension 0, may hold values from -100 to 100
- values: bfloat16 [16384, 5120], P(('expert', 'seq', 'fsdp')), parts along dimension 0, may hold values from -6 to 6
- query_gain: float32 [10240], P('expert'), parts along dimension 0, may hold values from 1 to 3
- key_gain: float32 [10240], P('expert'), parts along dimension 0, may hold values from 1 to 3
- timestep: int32 [2], P('expert'), parts along dimension 0, may hold values from 0 to 999, as said below
- gate_base: float32 [10240], P('expert'), parts along dimension 0, may hold values from -3 to 3
- time_weight: float32 [512, 5120], P('expert'), parts along dimension 0, may hold values from -0.375 to 0.375
Outputs:
- attended: bfloat16 [16384, 5120], P(('expert', 'seq', 'fsdp')), parts along dimension 0
There are 2 independent parts, one for each index of `expert`. A program takes and returns all parts, laid end to end along the dimension named above; each array names one. Nothing has to cross between parts.
Inputs may be any that keep to these rules, and one draw needn't show every extreme that they name: Part 0 is the high-noise group, with a timestep from 875 to 999; part 1 the low-noise group, with one from 0 to 874.
All inputs are finite; a program needn't handle non-finite values.
Results may differ from a plain program's by a relative error of at most 0.012.
The roundings to bfloat16 on the way count: a program that leaves them out, or rounds other values in their place, can miss the bound.
Values may be sent and summed in bfloat16 or wider, within the bound.
A program may use at most 384 MiB of HBM per device.

v0:
```python
import math
import jax
import jax.numpy as jnp
from jax import lax
from jax.sharding import PartitionSpec as P

HEAD_DIM = 128
FREQ = 256
HGT = 32
WID = 32
EPSILON = 1e-06


def rms_normed(tensor, gain_vector):
    mean_square = jnp.mean(tensor * tensor, axis=-1, keepdims=True)
    return tensor * lax.rsqrt(mean_square + EPSILON) * gain_vector


def rotate_pairs(tensor, positions):
    half_dim = HEAD_DIM // 2
    sixth = HEAD_DIM // 6
    frame_pairs = (HEAD_DIM - 4 * sixth) // 2
    pair_index = jnp.arange(half_dim, dtype=jnp.int32)
    in_frame = pair_index < frame_pairs
    in_height = (pair_index >= frame_pairs) & (pair_index < frame_pairs + sixth)
    local_index = jnp.where(
        in_frame,
        pair_index,
        jnp.where(in_height, pair_index - frame_pairs, pair_index - frame_pairs - sixth),
    )
    segment_dims = jnp.where(in_frame, 2 * frame_pairs, 2 * sixth)
    inverse = jnp.power(
        jnp.float32(10000.0),
        -2.0 * local_index.astype(jnp.float32) / segment_dims.astype(jnp.float32),
    )
    frame_at = positions // (HGT * WID)
    height_at = positions // WID % HGT
    width_at = positions % WID
    coordinate = jnp.where(
        in_frame[None, :],
        frame_at[:, None],
        jnp.where(in_height[None, :], height_at[:, None], width_at[:, None]),
    ).astype(jnp.float32)
    angle_table = coordinate * inverse[None, :]
    cosine = jnp.cos(angle_table)[:, None, :]
    sine_table = jnp.sin(angle_table)[:, None, :]
    paired = tensor.reshape(tensor.shape[0], tensor.shape[1], half_dim, 2)
    even_part = paired[..., 0]
    odd_part = paired[..., 1]
    turned = jnp.stack(
        [even_part * cosine - odd_part * sine_table, even_part * sine_table + odd_part * cosine],
        axis=-1,
    )
    return turned.reshape(tensor.shape)


def prepare(tensor, gain_vector, positions):
    normed = rms_normed(tensor.astype(jnp.float32), gain_vector)
    head_total = tensor.shape[1] // HEAD_DIM
    turned = rotate_pairs(normed.reshape(tensor.shape[0], head_total, HEAD_DIM), positions)
    return turned.reshape(tensor.shape).astype(jnp.bfloat16)


def gate_vector(timestep, base_slice, weight_slice):
    half_freq = FREQ // 2
    exponent = jnp.arange(half_freq, dtype=jnp.int32).astype(jnp.float32) / half_freq
    frequency = jnp.power(jnp.float32(10000.0), -exponent)
    phase = timestep.astype(jnp.float32)[:, None] * frequency[None, :]
    embedded = jnp.concatenate([jnp.cos(phase), jnp.sin(phase)], axis=1)
    projected = jnp.dot(
        embedded, weight_slice, precision=lax.Precision.HIGHEST, preferred_element_type=jnp.float32
    )
    return base_slice + projected[0]


def initial_state(query_count, heads_here):
    running_max = jnp.full((heads_here, query_count), -1e30, jnp.float32)
    running_total = jnp.zeros((heads_here, query_count), jnp.float32)
    accumulated = jnp.zeros((query_count, heads_here, HEAD_DIM), jnp.float32)
    return (running_max, running_total, accumulated)


def attend_keys(softmax_state, query_heads, key_piece, value_piece):
    query_count = query_heads.shape[0]
    heads_here = query_heads.shape[1] // HEAD_DIM
    query_view = query_heads.reshape(query_count, heads_here, HEAD_DIM)
    key_count = key_piece.shape[0]
    block_size = math.gcd(key_count, 1024)
    key_view = key_piece.reshape(key_count // block_size, block_size, heads_here, HEAD_DIM)
    value_view = value_piece.reshape(key_count // block_size, block_size, heads_here, HEAD_DIM)
    score_scale = 1.0 / math.sqrt(HEAD_DIM)

    def advance(running, blocks):
        running_max, running_total, accumulated = running
        key_block, value_block = blocks
        scores = (
            jnp.einsum("qhd,khd->hqk", query_view, key_block, preferred_element_type=jnp.float32)
            * score_scale
        )
        new_max = jnp.maximum(running_max, jnp.max(scores, axis=2))
        shrink = jnp.exp(running_max - new_max)
        exponent_values = jnp.exp(scores - new_max[:, :, None])
        new_total = running_total * shrink + jnp.sum(exponent_values, axis=2)
        weights = exponent_values.astype(jnp.bfloat16)
        update = jnp.einsum(
            "hqk,khd->qhd", weights, value_block, preferred_element_type=jnp.float32
        )
        new_accumulated = accumulated * jnp.transpose(shrink)[:, :, None] + update
        return ((new_max, new_total, new_accumulated), None)

    softmax_state, unused = lax.scan(advance, softmax_state, (key_view, value_view))
    return softmax_state


def local(queries, keys, values, query_gain, key_gain, timestep, gate_base, time_weight):
    token_count = queries.shape[0]
    width_total = queries.shape[1]
    seq_count = lax.axis_size("seq")
    fsdp_count = lax.axis_size("fsdp")
    block_index = lax.axis_index("seq") * fsdp_count + lax.axis_index("fsdp")
    positions = block_index * token_count + jnp.arange(token_count, dtype=jnp.int32)
    query_rot = prepare(queries, query_gain, positions)
    key_rot = prepare(keys, key_gain, positions)
    group_width = width_total // seq_count
    heads_here = group_width // HEAD_DIM
    group_start = lax.axis_index("seq") * group_width
    base_slice = lax.dynamic_slice_in_dim(gate_base, group_start, group_width, 0)
    weight_slice = lax.dynamic_slice_in_dim(time_weight, group_start, group_width, 1)
    gate_slice = gate_vector(timestep, base_slice, weight_slice)
    query_heads, key_heads, value_heads = (
        lax.all_to_all(query_rot, "seq", split_axis=1, concat_axis=0, tiled=True),
        lax.all_to_all(key_rot, "seq", split_axis=1, concat_axis=0, tiled=True),
        lax.all_to_all(values, "seq", split_axis=1, concat_axis=0, tiled=True),
    )
    softmax_state = initial_state(query_heads.shape[0], heads_here)
    softmax_state = attend_keys(
        softmax_state,
        query_heads,
        lax.all_gather(key_heads, "fsdp", axis=0, tiled=True),
        lax.all_gather(value_heads, "fsdp", axis=0, tiled=True),
    )
    running_max, running_total, accumulated = softmax_state
    heads_out = accumulated / jnp.transpose(running_total)[:, :, None]
    gated = (heads_out.reshape(heads_out.shape[0], group_width) * gate_slice[None, :]).astype(
        jnp.bfloat16
    )
    return lax.all_to_all(gated, "seq", split_axis=0, concat_axis=1, tiled=True)


def solution(mesh):
    return jax.shard_map(
        local,
        mesh=mesh,
        in_specs=(
            P(("expert", "seq", "fsdp"), None),
            P(("expert", "seq", "fsdp"), None),
            P(("expert", "seq", "fsdp"), None),
            P("expert"),
            P("expert"),
            P("expert"),
            P("expert"),
            P("expert", None),
        ),
        out_specs=P(("expert", "seq", "fsdp"), None),
        check_vma=False,
    )
```

profile of v0, /device:TPU:0, one launch (start us, length us, event | category | flops | bytes accessed | tf_op | source)
XLA Modules:
  0.0 1656.6 jit_solution(9292958395011838681)
XLA Ops:
  132.2 123.6 %all_to_all.64 = bf16[512,4,1280]{0,2,1:T(8,128)(2,1)} all-to-all(bf16[512,4,1280]{0,2,1:T(8,128)(2,1)} %convert_element_type.71), channel_id=1, replica_groups=mesh['expert'=2,'seq'=4,'fsdp'=4] {'seq'}, dimensions={1} | all-to-all | bytes 10485760 | tf_op jit(solution)/shard_map/all_to_all | solution.py:132
  271.7 121.5 %all_to_all.65 = bf16[512,4,1280]{0,2,1:T(8,128)(2,1)} all-to-all(bf16[512,4,1280]{0,2,1:T(8,128)(2,1)} %bitcast.73), channel_id=1, replica_groups=mesh['expert'=2,'seq'=4,'fsdp'=4] {'seq'}, dimensions={1} | all-to-all | bytes 10485760 | tf_op jit(solution)/shard_map/all_to_all | solution.py:133
  432.6 110.6 %all-to-all-done.1 = bf16[512,4,1280]{0,2,1:T(8,128)(2,1)} async-done(((bf16[512,4,1280]{0,2,1:T(8,128)(2,1)}), bf16[512,4,1280]{0,2,1:T(8,128)(2,1)}, u32[]{:S(2)}, u32[]{:S(2)}) %all-to-all-start.1) | async-done | bytes 5242912 | tf_op jit(solution)/shard_map/all_to_all | solution.py:131
  569.5 40.7 %reshape.322 = bf16[8,1024,10,128]{3,2,1,0:T(8,128)(2,1)} reshape(bf16[8192,1280]{1,0:T(8,128)(2,1)} %all-gather.3.cloned.1.call-done) | data formatting | bytes 41943040 | tf_op jit(solution)/shard_map/reshape | solution.py:89
  632.9 40.7 %reshape.323 = bf16[8,1024,10,128]{3,2,1,0:T(8,128)(2,1)} reshape(bf16[8192,1280]{1,0:T(8,128)(2,1)} %all-gather.5.cloned.1.call-done) | data formatting | bytes 41943040 | tf_op jit(solution)/shard_map/reshape | solution.py:90
  673.6 43.1 %copy.59 = bf16[8,1024,10,128]{1,3,2,0:T(8,128)(2,1)} copy(bf16[8,1024,10,128]{3,2,1,0:T(8,128)(2,1)} %reshape.323) | data formatting | bytes 41943040
  716.7 753.8 %while.15 = (s32[]{:T(128)}, f32[10,2048]{1,0:T(8,128)S(1)}, f32[10,2048]{1,0:T(8,128)S(1)}, f32[2048,10,128]{0,2,1:T(8,128)}, bf16[8,1024,10,128]{3,1,2,0:T(8,1...) while((s32[]{:T(128)}, f32[10,2048]{1,0:T(8,128)S(1)}, ...), condition=%wide.region_5.6_spmd.clone, body=%wide.region_2.5_spmd.clone.sunk | while | flops 10913177600 | bytes 284427360 | solution.py:111
  716.7 31.8 %bitcast_reduce_fusion.2 = (f32[10,2048]{1,0:T(8,128)S(1)}, f32[10,1024,2048]{2,1,0:T(8,128)}) fusion(bf16[2048,10,128]{2,0,1:T(8,128)(2,1)} %get-tuple-element.203, bf16[8,1024,10,128]{3,1,2,0:T(8,128)(2,1)} %get-tuple-element.202, s32[]{:T(128)} %get-tuple-element.189), kind=kOutput, calls=%fused_computation.1.clone.1 | convolution fusion | flops 5410631680 | bytes 91832832 | tf_op jit(solution)/shard_map/while/body/eval_jaxpr/qhd,khd->hqk/dot_general | solution.py:97
  748.5 33.6 %bitcast_add_fusion.2 = f32[2048,10,128]{0,2,1:T(8,128)} fusion(f32[2048,10,128]{0,2,1:T(8,128)} %get-tuple-element.192, f32[2048,10]{0,1:T(8,128)S(1)} %get-tuple-element.179, pred[]{:T(512)S(6)} %compare.24, f32[10,1024,2048]{2,1,0:T(8,128)} %get-tuple-element.178, f32[10,2048]{1,0:T(8,128)S(1)} %get-tuple-element.199, ...), kind=kOutput, calls=%fused_computation.8.clone.1 | convolution fusion | flops 5439488000 | bytes 107643392 | tf_op jit(solution)/shard_map/while/body/eval_jaxpr/hqk,khd->qhd/dot_general | solution.py:105
  808.3 31.8 %bitcast_reduce_fusion.2 = (f32[10,2048]{1,0:T(8,128)S(1)}, f32[10,1024,2048]{2,1,0:T(8,128)}) fusion(bf16[2048,10,128]{2,0,1:T(8,128)(2,1)} %get-tuple-element.203, bf16[8,1024,10,128]{3,1,2,0:T(8,128)(2,1)} %get-tuple-element.202, s32[]{:T(128)} %get-tuple-element.189), kind=kOutput, calls=%fused_computation.1.clone.1 | convolution fusion | flops 5410631680 | bytes 91832832 | tf_op jit(solution)/shard_map/while/body/eval_jaxpr/qhd,khd->hqk/dot_general | solution.py:97
  840.1 36.5 %bitcast_add_fusion.2 = f32[2048,10,128]{0,2,1:T(8,128)} fusion(f32[2048,10,128]{0,2,1:T(8,128)} %get-tuple-element.192, f32[2048,10]{0,1:T(8,128)S(1)} %get-tuple-element.179, pred[]{:T(512)S(6)} %compare.24, f32[10,1024,2048]{2,1,0:T(8,128)} %get-tuple-element.178, f32[10,2048]{1,0:T(8,128)S(1)} %get-tuple-element.199, ...), kind=kOutput, calls=%fused_computation.8.clone.1 | convolution fusion | flops 5439488000 | bytes 107643392 | tf_op jit(solution)/shard_map/while/body/eval_jaxpr/hqk,khd->qhd/dot_general | solution.py:105
  902.8 31.8 %bitcast_reduce_fusion.2 = (f32[10,2048]{1,0:T(8,128)S(1)}, f32[10,1024,2048]{2,1,0:T(8,128)}) fusion(bf16[2048,10,128]{2,0,1:T(8,128)(2,1)} %get-tuple-element.203, bf16[8,1024,10,128]{3,1,2,0:T(8,128)(2,1)} %get-tuple-element.202, s32[]{:T(128)} %get-tuple-element.189), kind=kOutput, calls=%fused_computation.1.clone.1 | convolution fusion | flops 5410631680 | bytes 91832832 | tf_op jit(solution)/shard_map/while/body/eval_jaxpr/qhd,khd->hqk/dot_general | solution.py:97
  934.7 36.5 %bitcast_add_fusion.2 = f32[2048,10,128]{0,2,1:T(8,128)} fusion(f32[2048,10,128]{0,2,1:T(8,128)} %get-tuple-element.192, f32[2048,10]{0,1:T(8,128)S(1)} %get-tuple-element.179, pred[]{:T(512)S(6)} %compare.24, f32[10,1024,2048]{2,1,0:T(8,128)} %get-tuple-element.178, f32[10,2048]{1,0:T(8,128)S(1)} %get-tuple-element.199, ...), kind=kOutput, calls=%fused_computation.8.clone.1 | convolution fusion | flops 5439488000 | bytes 107643392 | tf_op jit(solution)/shard_map/while/body/eval_jaxpr/hqk,khd->qhd/dot_general | solution.py:105
  997.4 31.8 %bitcast_reduce_fusion.2 = (f32[10,2048]{1,0:T(8,128)S(1)}, f32[10,1024,2048]{2,1,0:T(8,128)}) fusion(bf16[2048,10,128]{2,0,1:T(8,128)(2,1)} %get-tuple-element.203, bf16[8,1024,10,128]{3,1,2,0:T(8,128)(2,1)} %get-tuple-element.202, s32[]{:T(128)} %get-tuple-element.189), kind=kOutput, calls=%fused_computation.1.clone.1 | convolution fusion | flops 5410631680 | bytes 91832832 | tf_op jit(solution)/shard_map/while/body/eval_jaxpr/qhd,khd->hqk/dot_general | solution.py:97
  1029.3 36.5 %bitcast_add_fusion.2 = f32[2048,10,128]{0,2,1:T(8,128)} fusion(f32[2048,10,128]{0,2,1:T(8,128)} %get-tuple-element.192, f32[2048,10]{0,1:T(8,128)S(1)} %get-tuple-element.179, pred[]{:T(512)S(6)} %compare.24, f32[10,1024,2048]{2,1,0:T(8,128)} %get-tuple-element.178, f32[10,2048]{1,0:T(8,128)S(1)} %get-tuple-element.199, ...), kind=kOutput, calls=%fused_computation.8.clone.1 | convolution fusion | flops 5439488000 | bytes 107643392 | tf_op jit(solution)/shard_map/while/body/eval_jaxpr/hqk,khd->qhd/dot_general | solution.py:105
  1092.0 31.8 %bitcast_reduce_fusion.2 = (f32[10,2048]{1,0:T(8,128)S(1)}, f32[10,1024,2048]{2,1,0:T(8,128)}) fusion(bf16[2048,10,128]{2,0,1:T(8,128)(2,1)} %get-tuple-element.203, bf16[8,1024,10,128]{3,1,2,0:T(8,128)(2,1)} %get-tuple-element.202, s32[]{:T(128)} %get-tuple-element.189), kind=kOutput, calls=%fused_computation.1.clone.1 | convolution fusion | flops 5410631680 | bytes 91832832 | tf_op jit(solution)/shard_map/while/body/eval_jaxpr/qhd,khd->hqk/dot_general | solution.py:97
  1123.8 36.5 %bitcast_add_fusion.2 = f32[2048,10,128]{0,2,1:T(8,128)} fusion(f32[2048,10,128]{0,2,1:T(8,128)} %get-tuple-element.192, f32[2048,10]{0,1:T(8,128)S(1)} %get-tuple-element.179, pred[]{:T(512)S(6)} %compare.24, f32[10,1024,2048]{2,1,0:T(8,128)} %get-tuple-element.178, f32[10,2048]{1,0:T(8,128)S(1)} %get-tuple-element.199, ...), kind=kOutput, calls=%fused_computation.8.clone.1 | convolution fusion | flops 5439488000 | bytes 107643392 | tf_op jit(solution)/shard_map/while/body/eval_jaxpr/hqk,khd->qhd/dot_general | solution.py:105
  1186.6 31.8 %bitcast_reduce_fusion.2 = (f32[10,2048]{1,0:T(8,128)S(1)}, f32[10,1024,2048]{2,1,0:T(8,128)}) fusion(bf16[2048,10,128]{2,0,1:T(8,128)(2,1)} %get-tuple-element.203, bf16[8,1024,10,128]{3,1,2,0:T(8,128)(2,1)} %get-tuple-element.202, s32[]{:T(128)} %get-tuple-element.189), kind=kOutput, calls=%fused_computation.1.clone.1 | convolution fusion | flops 5410631680 | bytes 91832832 | tf_op jit(solution)/shard_map/while/body/eval_jaxpr/qhd,khd->hqk/dot_general | solution.py:97
  1218.4 36.5 %bitcast_add_fusion.2 = f32[2048,10,128]{0,2,1:T(8,128)} fusion(f32[2048,10,128]{0,2,1:T(8,128)} %get-tuple-element.192, f32[2048,10]{0,1:T(8,128)S(1)} %get-tuple-element.179, pred[]{:T(512)S(6)} %compare.24, f32[10,1024,2048]{2,1,0:T(8,128)} %get-tuple-element.178, f32[10,2048]{1,0:T(8,128)S(1)} %get-tuple-element.199, ...), kind=kOutput, calls=%fused_computation.8.clone.1 | convolution fusion | flops 5439488000 | bytes 107643392 | tf_op jit(solution)/shard_map/while/body/eval_jaxpr/hqk,khd->qhd/dot_general | solution.py:105
  1281.1 31.8 %bitcast_reduce_fusion.2 = (f32[10,2048]{1,0:T(8,128)S(1)}, f32[10,1024,2048]{2,1,0:T(8,128)}) fusion(bf16[2048,10,128]{2,0,1:T(8,128)(2,1)} %get-tuple-element.203, bf16[8,1024,10,128]{3,1,2,0:T(8,128)(2,1)} %get-tuple-element.202, s32[]{:T(128)} %get-tuple-element.189), kind=kOutput, calls=%fused_computation.1.clone.1 | convolution fusion | flops 5410631680 | bytes 91832832 | tf_op jit(solution)/shard_map/while/body/eval_jaxpr/qhd,khd->hqk/dot_general | solution.py:97
  1313.0 36.5 %bitcast_add_fusion.2 = f32[2048,10,128]{0,2,1:T(8,128)} fusion(f32[2048,10,128]{0,2,1:T(8,128)} %get-tuple-element.192, f32[2048,10]{0,1:T(8,128)S(1)} %get-tuple-element.179, pred[]{:T(512)S(6)} %compare.24, f32[10,1024,2048]{2,1,0:T(8,128)} %get-tuple-element.178, f32[10,2048]{1,0:T(8,128)S(1)} %get-tuple-element.199, ...), kind=kOutput, calls=%fused_computation.8.clone.1 | convolution fusion | flops 5439488000 | bytes 107643392 | tf_op jit(solution)/shard_map/while/body/eval_jaxpr/hqk,khd->qhd/dot_general | solution.py:105
  1375.7 31.8 %bitcast_reduce_fusion.2 = (f32[10,2048]{1,0:T(8,128)S(1)}, f32[10,1024,2048]{2,1,0:T(8,128)}) fusion(bf16[2048,10,128]{2,0,1:T(8,128)(2,1)} %get-tuple-element.203, bf16[8,1024,10,128]{3,1,2,0:T(8,128)(2,1)} %get-tuple-element.202, s32[]{:T(128)} %get-tuple-element.189), kind=kOutput, calls=%fused_computation.1.clone.1 | convolution fusion | flops 5410631680 | bytes 91832832 | tf_op jit(solution)/shard_map/while/body/eval_jaxpr/qhd,khd->hqk/dot_general | solution.py:97
  1407.6 36.5 %bitcast_add_fusion.2 = f32[2048,10,128]{0,2,1:T(8,128)} fusion(f32[2048,10,128]{0,2,1:T(8,128)} %get-tuple-element.192, f32[2048,10]{0,1:T(8,128)S(1)} %get-tuple-element.179, pred[]{:T(512)S(6)} %compare.24, f32[10,1024,2048]{2,1,0:T(8,128)} %get-tuple-element.178, f32[10,2048]{1,0:T(8,128)S(1)} %get-tuple-element.199, ...), kind=kOutput, calls=%fused_computation.8.clone.1 | convolution fusion | flops 5439488000 | bytes 107643392 | tf_op jit(solution)/shard_map/while/body/eval_jaxpr/hqk,khd->qhd/dot_general | solution.py:105
  1512.8 121.2 %all_to_all.66 = bf16[4,512,1280]{2,1,0:T(8,128)(2,1)} all-to-all(bf16[4,512,1280]{2,1,0:T(8,128)(2,1)} %copy.60), channel_id=1, replica_groups=mesh['expert'=2,'seq'=4,'fsdp'=4] {'seq'}, dimensions={0} | all-to-all | bytes 10485760 | tf_op jit(solution)/shard_map/all_to_all | solution.py:147
  (82 shorter events, 496.7 us)
Async XLA Ops:
  6.5 563.0 %all-gather.3.cloned.1.call-start = ((), (), s32[]{:S(2)}) async-start(), calls=%async_computation.4 | async-start | bytes 26214400 | tf_op jit(solution)/shard_map/all_gather | solution.py:139
  29.7 16.5 copy-start.1
  263.7 369.2 %all-gather.5.cloned.1.call-start = ((), (), s32[]{:S(2)}) async-start(), calls=%async_computation.5 | async-start | bytes 26214400 | tf_op jit(solution)/shard_map/all_gather | solution.py:140
  423.3 119.9 %all-to-all-start.1 = ((bf16[512,4,1280]{0,2,1:T(8,128)(2,1)}), bf16[512,4,1280]{0,2,1:T(8,128)(2,1)}, u32[]{:S(2)}, u32[]{:S(2)}) async-start(bf16[512,4,1280]{0,2,1:T(8,128)(2,1)} %convert_element_type.73), calls=%async_computation.1 | async-start | bytes 10485760 | tf_op jit(solution)/shard_map/all_to_all | solution.py:131
  1480.8 13.2 copy-start
Sparse Core Ops, SparseCore 0:
  263.8 130.5 all-gather.2
  401.3 130.5 all-gather.4
where the time goes:
time: 1660 us
  matrix products  546 us (33%)
  blocking collectives  366 us (22%)
  other arithmetic  312 us (19%)
  local copies, waits for them, and re-layouts  302 us (18%)
  waiting for transfers between devices  111 us (7%)
    dot_general x8, matrix products, advance(): jnp.einsum('hqk,khd->qhd', weights, value_block, preferred_element_type=j...  289 us
    dot_general x8, matrix products, advance(): jnp.einsum('qhd,khd->hqk', query_view, key_block, preferred_element_type=...  255 us
    reduce_sum x8, other arithmetic, advance(): new_total = running_total * shrink + jnp.sum(exponent_values, axis=2)  209 us
    all_to_all x1, blocking collectives, local(): lax.all_to_all(key_rot, 'seq', split_axis=1, concat_axis=0, tiled=True)  124 us
    all_to_all x1, blocking collectives, local(): lax.all_to_all(values, 'seq', split_axis=1, concat_axis=0, tiled=True)  122 us
    all_to_all x1, blocking collectives, local(): return lax.all_to_all(gated, 'seq', split_axis=0, concat_axis=1, tiled=True)  121 us
    all_to_all x1, waiting for transfers between devices, local(): lax.all_to_all(query_rot, 'seq', split_axis=1, concat_axis=0, tiled=True)  111 us
    unnamed x8, local copies, waits for them, and re-layouts  81.6 us
  transfers between devices with their start and end apart: 3, of which 1 were waited for; matrix products, arithmetic and copies ran while one was open for 8% of the time, Pallas kernels for 0%

commit v1 on v0

--- a/solution.py
+++ b/solution.py
@@ -9,6 +9,22 @@
 HGT = 32
 WID = 32
 EPSILON = 1e-06
+
+
+def exchange_in_pairs(value, axis, split, join):
+    ways, here = (lax.axis_size(axis), lax.axis_index(axis))
+    width = value.shape[split] // ways
+    dims = list(value.shape)
+    dims[split] = width
+    height = dims[join]
+    dims[join] = height * ways
+    full = jnp.zeros(dims, value.dtype)
+    for mask in range(ways):
+        part = lax.dynamic_slice_in_dim(value, (here ^ mask) * width, width, axis=split)
+        if mask:
+            part = lax.ppermute(part, axis, [(d, d ^ mask) for d in range(ways)])
+        full = lax.dynamic_update_slice_in_dim(full, part, (here ^ mask) * height, axis=join)
+    return full
 
 
 def rms_normed(tensor, gain_vector):
@@ -130,7 +146,7 @@
     query_heads, key_heads, value_heads = (
         lax.all_to_all(query_rot, "seq", split_axis=1, concat_axis=0, tiled=True),
         lax.all_to_all(key_rot, "seq", split_axis=1, concat_axis=0, tiled=True),
-        lax.all_to_all(values, "seq", split_axis=1, concat_axis=0, tiled=True),
+        exchange_in_pairs(values, "seq", 1, 0),
     )
     softmax_state = initial_state(query_heads.shape[0], heads_here)
     softmax_state = attend_keys(

time: 1660 us -> 1610 us (0.970)
  blocking collectives: 366 us -> 263 us
  waiting for transfers between devices: 111 us -> 192 us
  local copies, waits for them, and re-layouts: 302 us -> 266 us
    all_to_all x1 -> x0, blocking collectives: 122 us -> none  [local(): lax.all_to_all(values, 'seq', split_axis=1, concat_axis=0, tiled=True)]
    ppermute x0 -> x3, waiting for transfers between devices: none -> 79.9 us  [exchange_in_pairs(): part = lax.ppermute(part, axis, [(d, d ^ mask) for d in range(ways)])]
    reshape x1 -> x0, local copies, waits for them, and re-layouts: 40.7 us -> none  [attend_keys(): value_piece.reshape(key_count // block_size, block_size, heads_here, HEAD...]
    all_to_all x1, blocking collectives: 124 us -> 142 us  [local(): lax.all_to_all(key_rot, 'seq', split_axis=1, concat_axis=0, tiled=True)]
    unnamed x8 -> x10, local copies, waits for them, and re-layouts: 81.6 us -> 75.7 us
  transfers between devices with their start and end apart: 3 -> 6, of which waited for: 1 -> 3; matrix products, arithmetic and copies ran while one was open for 8% -> 15% of each run, Pallas kernels for 0% -> 0%
where the time goes in v1:
time: 1610 us
  matrix products  546 us (34%)
  other arithmetic  314 us (20%)
  local copies, waits for them, and re-layouts  266 us (17%)
  blocking collectives  263 us (16%)
  waiting for transfers between devices  192 us (12%)
    dot_general x8, matrix products, advance(): jnp.einsum('hqk,khd->qhd', weights, value_block, preferred_element_type=j...  289 us
    dot_general x8, matrix products, advance(): jnp.einsum('qhd,khd->hqk', query_view, key_block, preferred_element_type=...  255 us
    reduce_sum x8, other arithmetic, advance(): new_total = running_total * shrink + jnp.sum(exponent_values, axis=2)  209 us
    all_to_all x1, blocking collectives, local(): lax.all_to_all(key_rot, 'seq', split_axis=1, concat_axis=0, tiled=True)  142 us
    all_to_all x1, blocking collectives, local(): return lax.all_to_all(gated, 'seq', split_axis=0, concat_axis=1, tiled=True)  121 us
    all_to_all x1, waiting for transfers between devices, local(): lax.all_to_all(query_rot, 'seq', split_axis=1, concat_axis=0, tiled=True)  112 us
    ppermute x3, waiting for transfers between devices, exchange_in_pairs(): part = lax.ppermute(part, axis, [(d, d ^ mask) for d in range(ways)])  79.9 us
    unnamed x10, local copies, waits for them, and re-layouts  75.7 us
  transfers between devices with their start and end apart: 6, of which 3 were waited for; matrix products, arithmetic and copies ran while one was open for 15% of the time, Pallas kernels for 0%

profile of v1, /device:TPU:0, one launch (start us, length us, event | category | flops | bytes accessed | tf_op | source)
XLA Modules:
  0.0 1607.0 jit_solution(10574533252239122612)
XLA Ops:
  21.6 48.9 %collective-permute-done = bf16[512,1280]{1,0:T(8,128)(2,1)} collective-permute-done((bf16[512,1280]{1,0:T(8,128)(2,1)}, bf16[512,1280]{1,0:T(8,128)(2,1)}, u32[]{:S(2)}, u32[]{:S(2)}) %collective-permute-start) | collective-permute-done | bytes 1310752 | tf_op jit(solution)/shard_map/ppermute | solution.py:25
  72.2 31.0 %collective-permute-done.1 = bf16[512,1280]{1,0:T(8,128)(2,1)} collective-permute-done((bf16[512,1280]{1,0:T(8,128)(2,1)}, bf16[512,1280]{1,0:T(8,128)(2,1)}, u32[]{:S(2)}, u32[]{:S(2)}) %collective-permute-start.1) | collective-permute-done | bytes 1310752 | tf_op jit(solution)/shard_map/ppermute | solution.py:25
  185.8 31.5 %subtract_convert_fusion = (bf16[512,40,64,1]{0,3,2,1:T(2,128)(2,1)}, bf16[512,40,64,1]{0,3,2,1:T(2,128)(2,1)}, bf16[512,40,64,1]{0,3,2,1:T(2,128)(2,1)}, bf16[512,40,64,1]{0,3,2,1:T(2,128)(2,1)}) fusion(f32[512,40,64,2]{0,3,2,1:T(2,128)} %reshape_reshape.9, f32[512,64]{0,1:T(8,128)S(1)} %get-tuple-element.119, f32[512,64]{0,1:T(8,128)S(1)} %get-tuple-element.118, ...), kind=kLoop, calls=%fused_computation.36 | loop fusion | flops 20971520 | bytes 31719424 | tf_op jit(solution)/shard_map/convert
  239.1 141.8 %all_to_all.45 = bf16[512,4,1280]{0,2,1:T(8,128)(2,1)} all-to-all(bf16[512,4,1280]{0,2,1:T(8,128)(2,1)} %convert_element_type.71), channel_id=1, replica_groups=mesh['expert'=2,'seq'=4,'fsdp'=4] {'seq'}, dimensions={1} | all-to-all | bytes 10485760 | tf_op jit(solution)/shard_map/all_to_all | solution.py:148
  420.2 111.7 %all-to-all-done.1 = bf16[512,4,1280]{0,2,1:T(8,128)(2,1)} async-done(((bf16[512,4,1280]{0,2,1:T(8,128)(2,1)}), bf16[512,4,1280]{0,2,1:T(8,128)(2,1)}, u32[]{:S(2)}, u32[]{:S(2)}) %all-to-all-start.1) | async-done | bytes 5242912 | tf_op jit(solution)/shard_map/all_to_all | solution.py:147
  603.5 40.7 %reshape.319 = bf16[8,1024,10,128]{3,2,1,0:T(8,128)(2,1)} reshape(bf16[8192,1280]{1,0:T(8,128)(2,1)} %all-gather.3.cloned.1.call-done) | data formatting | bytes 41943040 | tf_op jit(solution)/shard_map/reshape | solution.py:105
  666.8 754.0 %while.15 = (s32[]{:T(128)}, f32[10,2048]{1,0:T(8,128)S(1)}, f32[10,2048]{1,0:T(8,128)S(1)}, f32[2048,10,128]{0,2,1:T(8,128)}, bf16[8,1024,10,128]{3,1,2,0:T(8,1...) while((s32[]{:T(128)}, f32[10,2048]{1,0:T(8,128)S(1)}, ...), condition=%wide.region_5.6_spmd.clone, body=%wide.region_2.5_spmd.clone.sunk | while | flops 10913177600 | bytes 284427360 | solution.py:127
  666.8 31.8 %bitcast_reduce_fusion.2 = (f32[10,2048]{1,0:T(8,128)S(1)}, f32[10,1024,2048]{2,1,0:T(8,128)}) fusion(bf16[2048,10,128]{2,0,1:T(8,128)(2,1)} %get-tuple-element.200, bf16[8,1024,10,128]{3,1,2,0:T(8,128)(2,1)} %get-tuple-element.199, s32[]{:T(128)} %get-tuple-element.186), kind=kOutput, calls=%fused_computation.1.clone.1 | convolution fusion | flops 5410631680 | bytes 91832832 | tf_op jit(solution)/shard_map/while/body/eval_jaxpr/qhd,khd->hqk/dot_general | solution.py:113
  698.7 33.6 %bitcast_add_fusion.2 = f32[2048,10,128]{0,2,1:T(8,128)} fusion(f32[2048,10,128]{0,2,1:T(8,128)} %get-tuple-element.189, f32[2048,10]{0,1:T(8,128)S(1)} %get-tuple-element.176, pred[]{:T(512)S(6)} %compare.24, f32[10,1024,2048]{2,1,0:T(8,128)} %get-tuple-element.175, f32[10,2048]{1,0:T(8,128)S(1)} %get-tuple-element.196, ...), kind=kOutput, calls=%fused_computation.8.clone.1 | convolution fusion | flops 5439488000 | bytes 107643392 | tf_op jit(solution)/shard_map/while/body/eval_jaxpr/hqk,khd->qhd/dot_general | solution.py:121
  758.5 31.8 %bitcast_reduce_fusion.2 = (f32[10,2048]{1,0:T(8,128)S(1)}, f32[10,1024,2048]{2,1,0:T(8,128)}) fusion(bf16[2048,10,128]{2,0,1:T(8,128)(2,1)} %get-tuple-element.200, bf16[8,1024,10,128]{3,1,2,0:T(8,128)(2,1)} %get-tuple-element.199, s32[]{:T(128)} %get-tuple-element.186), kind=kOutput, calls=%fused_computation.1.clone.1 | convolution fusion | flops 5410631680 | bytes 91832832 | tf_op jit(solution)/shard_map/while/body/eval_jaxpr/qhd,khd->hqk/dot_general | solution.py:113
  790.3 36.5 %bitcast_add_fusion.2 = f32[2048,10,128]{0,2,1:T(8,128)} fusion(f32[2048,10,128]{0,2,1:T(8,128)} %get-tuple-element.189, f32[2048,10]{0,1:T(8,128)S(1)} %get-tuple-element.176, pred[]{:T(512)S(6)} %compare.24, f32[10,1024,2048]{2,1,0:T(8,128)} %get-tuple-element.175, f32[10,2048]{1,0:T(8,128)S(1)} %get-tuple-element.196, ...), kind=kOutput, calls=%fused_computation.8.clone.1 | convolution fusion | flops 5439488000 | bytes 107643392 | tf_op jit(solution)/shard_map/while/body/eval_jaxpr/hqk,khd->qhd/dot_general | solution.py:121
  853.1 31.8 %bitcast_reduce_fusion.2 = (f32[10,2048]{1,0:T(8,128)S(1)}, f32[10,1024,2048]{2,1,0:T(8,128)}) fusion(bf16[2048,10,128]{2,0,1:T(8,128)(2,1)} %get-tuple-element.200, bf16[8,1024,10,128]{3,1,2,0:T(8,128)(2,1)} %get-tuple-element.199, s32[]{:T(128)} %get-tuple-element.186), kind=kOutput, calls=%fused_computation.1.clone.1 | convolution fusion | flops 5410631680 | bytes 91832832 | tf_op jit(solution)/shard_map/while/body/eval_jaxpr/qhd,khd->hqk/dot_general | solution.py:113
  885.0 36.5 %bitcast_add_fusion.2 = f32[2048,10,128]{0,2,1:T(8,128)} fusion(f32[2048,10,128]{0,2,1:T(8,128)} %get-tuple-element.189, f32[2048,10]{0,1:T(8,128)S(1)} %get-tuple-element.176, pred[]{:T(512)S(6)} %compare.24, f32[10,1024,2048]{2,1,0:T(8,128)} %get-tuple-element.175, f32[10,2048]{1,0:T(8,128)S(1)} %get-tuple-element.196, ...), kind=kOutput, calls=%fused_computation.8.clone.1 | convolution fusion | flops 5439488000 | bytes 107643392 | tf_op jit(solution)/shard_map/while/body/eval_jaxpr/hqk,khd->qhd/dot_general | solution.py:121
  947.7 31.8 %bitcast_reduce_fusion.2 = (f32[10,2048]{1,0:T(8,128)S(1)}, f32[10,1024,2048]{2,1,0:T(8,128)}) fusion(bf16[2048,10,128]{2,0,1:T(8,128)(2,1)} %get-tuple-element.200, bf16[8,1024,10,128]{3,1,2,0:T(8,128)(2,1)} %get-tuple-element.199, s32[]{:T(128)} %get-tuple-element.186), kind=kOutput, calls=%fused_computation.1.clone.1 | convolution fusion | flops 5410631680 | bytes 91832832 | tf_op jit(solution)/shard_map/while/body/eval_jaxpr/qhd,khd->hqk/dot_general | solution.py:113
  979.6 36.5 %bitcast_add_fusion.2 = f32[2048,10,128]{0,2,1:T(8,128)} fusion(f32[2048,10,128]{0,2,1:T(8,128)} %get-tuple-element.189, f32[2048,10]{0,1:T(8,128)S(1)} %get-tuple-element.176, pred[]{:T(512)S(6)} %compare.24, f32[10,1024,2048]{2,1,0:T(8,128)} %get-tuple-element.175, f32[10,2048]{1,0:T(8,128)S(1)} %get-tuple-element.196, ...), kind=kOutput, calls=%fused_computation.8.clone.1 | convolution fusion | flops 5439488000 | bytes 107643392 | tf_op jit(solution)/shard_map/while/body/eval_jaxpr/hqk,khd->qhd/dot_general | solution.py:121
  1042.3 31.8 %bitcast_reduce_fusion.2 = (f32[10,2048]{1,0:T(8,128)S(1)}, f32[10,1024,2048]{2,1,0:T(8,128)}) fusion(bf16[2048,10,128]{2,0,1:T(8,128)(2,1)} %get-tuple-element.200, bf16[8,1024,10,128]{3,1,2,0:T(8,128)(2,1)} %get-tuple-element.199, s32[]{:T(128)} %get-tuple-element.186), kind=kOutput, calls=%fused_computation.1.clone.1 | convolution fusion | flops 5410631680 | bytes 91832832 | tf_op jit(solution)/shard_map/while/body/eval_jaxpr/qhd,khd->hqk/dot_general | solution.py:113
  1074.2 36.5 %bitcast_add_fusion.2 = f32[2048,10,128]{0,2,1:T(8,128)} fusion(f32[2048,10,128]{0,2,1:T(8,128)} %get-tuple-element.189, f32[2048,10]{0,1:T(8,128)S(1)} %get-tuple-element.176, pred[]{:T(512)S(6)} %compare.24, f32[10,1024,2048]{2,1,0:T(8,128)} %get-tuple-element.175, f32[10,2048]{1,0:T(8,128)S(1)} %get-tuple-element.196, ...), kind=kOutput, calls=%fused_computation.8.clone.1 | convolution fusion | flops 5439488000 | bytes 107643392 | tf_op jit(solution)/shard_map/while/body/eval_jaxpr/hqk,khd->qhd/dot_general | solution.py:121
  1137.0 31.8 %bitcast_reduce_fusion.2 = (f32[10,2048]{1,0:T(8,128)S(1)}, f32[10,1024,2048]{2,1,0:T(8,128)}) fusion(bf16[2048,10,128]{2,0,1:T(8,128)(2,1)} %get-tuple-element.200, bf16[8,1024,10,128]{3,1,2,0:T(8,128)(2,1)} %get-tuple-element.199, s32[]{:T(128)} %get-tuple-element.186), kind=kOutput, calls=%fused_computation.1.clone.1 | convolution fusion | flops 5410631680 | bytes 91832832 | tf_op jit(solution)/shard_map/while/body/eval_jaxpr/qhd,khd->hqk/dot_general | solution.py:113
  1168.8 36.5 %bitcast_add_fusion.2 = f32[2048,10,128]{0,2,1:T(8,128)} fusion(f32[2048,10,128]{0,2,1:T(8,128)} %get-tuple-element.189, f32[2048,10]{0,1:T(8,128)S(1)} %get-tuple-element.176, pred[]{:T(512)S(6)} %compare.24, f32[10,1024,2048]{2,1,0:T(8,128)} %get-tuple-element.175, f32[10,2048]{1,0:T(8,128)S(1)} %get-tuple-element.196, ...), kind=kOutput, calls=%fused_computation.8.clone.1 | convolution fusion | flops 5439488000 | bytes 107643392 | tf_op jit(solution)/shard_map/while/body/eval_jaxpr/hqk,khd->qhd/dot_general | solution.py:121
  1231.6 31.8 %bitcast_reduce_fusion.2 = (f32[10,2048]{1,0:T(8,128)S(1)}, f32[10,1024,2048]{2,1,0:T(8,128)}) fusion(bf16[2048,10,128]{2,0,1:T(8,128)(2,1)} %get-tuple-element.200, bf16[8,1024,10,128]{3,1,2,0:T(8,128)(2,1)} %get-tuple-element.199, s32[]{:T(128)} %get-tuple-element.186), kind=kOutput, calls=%fused_computation.1.clone.1 | convolution fusion | flops 5410631680 | bytes 91832832 | tf_op jit(solution)/shard_map/while/body/eval_jaxpr/qhd,khd->hqk/dot_general | solution.py:113
  1263.4 36.5 %bitcast_add_fusion.2 = f32[2048,10,128]{0,2,1:T(8,128)} fusion(f32[2048,10,128]{0,2,1:T(8,128)} %get-tuple-element.189, f32[2048,10]{0,1:T(8,128)S(1)} %get-tuple-element.176, pred[]{:T(512)S(6)} %compare.24, f32[10,1024,2048]{2,1,0:T(8,128)} %get-tuple-element.175, f32[10,2048]{1,0:T(8,128)S(1)} %get-tuple-element.196, ...), kind=kOutput, calls=%fused_computation.8.clone.1 | convolution fusion | flops 5439488000 | bytes 107643392 | tf_op jit(solution)/shard_map/while/body/eval_jaxpr/hqk,khd->qhd/dot_general | solution.py:121
  1326.2 31.8 %bitcast_reduce_fusion.2 = (f32[10,2048]{1,0:T(8,128)S(1)}, f32[10,1024,2048]{2,1,0:T(8,128)}) fusion(bf16[2048,10,128]{2,0,1:T(8,128)(2,1)} %get-tuple-element.200, bf16[8,1024,10,128]{3,1,2,0:T(8,128)(2,1)} %get-tuple-element.199, s32[]{:T(128)} %get-tuple-element.186), kind=kOutput, calls=%fused_computation.1.clone.1 | convolution fusion | flops 5410631680 | bytes 91832832 | tf_op jit(solution)/shard_map/while/body/eval_jaxpr/qhd,khd->hqk/dot_general | solution.py:113
  1358.1 36.5 %bitcast_add_fusion.2 = f32[2048,10,128]{0,2,1:T(8,128)} fusion(f32[2048,10,128]{0,2,1:T(8,128)} %get-tuple-element.189, f32[2048,10]{0,1:T(8,128)S(1)} %get-tuple-element.176, pred[]{:T(512)S(6)} %compare.24, f32[10,1024,2048]{2,1,0:T(8,128)} %get-tuple-element.175, f32[10,2048]{1,0:T(8,128)S(1)} %get-tuple-element.196, ...), kind=kOutput, calls=%fused_computation.8.clone.1 | convolution fusion | flops 5439488000 | bytes 107643392 | tf_op jit(solution)/shard_map/while/body/eval_jaxpr/hqk,khd->qhd/dot_general | solution.py:121
  1463.1 121.3 %all_to_all.46 = bf16[4,512,1280]{2,1,0:T(8,128)(2,1)} all-to-all(bf16[4,512,1280]{2,1,0:T(8,128)(2,1)} %copy.52), channel_id=1, replica_groups=mesh['expert'=2,'seq'=4,'fsdp'=4] {'seq'}, dimensions={0} | all-to-all | bytes 10485760 | tf_op jit(solution)/shard_map/all_to_all | solution.py:163
  (97 shorter events, 521.7 us)
Async XLA Ops:
  6.5 551.7 %all-gather.5.cloned.1.call-start = ((), (), s32[]{:S(2)}) async-start(), calls=%async_computation.4 | async-start | bytes 26214400 | tf_op jit(solution)/shard_map/all_gather | solution.py:156
  11.1 59.5 %collective-permute-start = (bf16[512,1280]{1,0:T(8,128)(2,1)}, bf16[512,1280]{1,0:T(8,128)(2,1)}, u32[]{:S(2)}, u32[]{:S(2)}) collective-permute-start(bf16[512,1280]{1,0:T(8,128)(2,1)} %get-tuple-element.113), channel_id=1, source_target_pairs={{0,4},{4,0},{8,12},{12,8},{1,5},{5,1},{9,13},{13,9},{2,6},{6,2},{1... | collective-permute-start | bytes 3932168 | tf_op jit(solution)/shard_map/ppermute | solution.py:25
  14.1 89.0 %collective-permute-start.1 = (bf16[512,1280]{1,0:T(8,128)(2,1)}, bf16[512,1280]{1,0:T(8,128)(2,1)}, u32[]{:S(2)}, u32[]{:S(2)}) collective-permute-start(bf16[512,1280]{1,0:T(8,128)(2,1)} %get-tuple-element.115), channel_id=1, source_target_pairs={{0,8},{4,12},{8,0},{12,4},{1,9},{5,13},{9,1},{13,5},{2,10},{6,14},... | collective-permute-start | bytes 3932168 | tf_op jit(solution)/shard_map/ppermute | solution.py:25
  16.7 90.5 %collective-permute-start.2 = (bf16[512,1280]{1,0:T(8,128)(2,1)}, bf16[512,1280]{1,0:T(8,128)(2,1)}, u32[]{:S(2)}, u32[]{:S(2)}) collective-permute-start(bf16[512,1280]{1,0:T(8,128)(2,1)} %get-tuple-element.112), channel_id=1, source_target_pairs={{0,12},{4,8},{8,4},{12,0},{1,13},{5,9},{9,5},{13,1},{2,14},{6,10},... | collective-permute-start | bytes 3932168 | tf_op jit(solution)/shard_map/ppermute | solution.py:25
  110.0 3.9 copy-start.1
  110.0 493.5 %all-gather.3.cloned.1.call-start = ((), (), s32[]{:S(2)}) async-start(), calls=%async_computation.3 | async-start | bytes 26214400 | tf_op jit(solution)/shard_map/all_gather | solution.py:155
  147.3 5.2 copy-start.2
  411.0 121.0 %all-to-all-start.1 = ((bf16[512,4,1280]{0,2,1:T(8,128)(2,1)}), bf16[512,4,1280]{0,2,1:T(8,128)(2,1)}, u32[]{:S(2)}, u32[]{:S(2)}) async-start(bf16[512,4,1280]{0,2,1:T(8,128)(2,1)} %convert_element_type.73), calls=%async_computation.1 | async-start | bytes 10485760 | tf_op jit(solution)/shard_map/all_to_all | solution.py:147
  1431.1 13.2 copy-start
Sparse Core Ops, SparseCore 0:
  110.1 153.5 all-gather.4
  389.0 129.8 all-gather.2
